TPU v7x, 32 devices: a whole 2x2x4 slice. The times are simulated.
32 devices in a mesh: dp: 4 (over z), row: 4 (over y, x), col: 2 (over core).
Axes of the slice: x: 2, y: 2, z: 4, core: 2. Of those that a mesh axis runs over, the one named last changes fastest.
Arguments:
- grad_parts: bfloat16 [4, 1, 4, 512, 10240], P('dp', None, 'row', None, 'col'), may hold values from -6 to 6
- params: float32 [1, 4, 512, 10240], P(None, 'row', 'dp', 'col'), may hold values from -6 to 6
- row_second: float32 [1, 4, 512], P(None, 'row'), may hold values from 0.1 to 90
- col_second: float32 [1, 10240], P(None, 'col'), may hold values from 0.02 to 100
Outputs:
- new_params: float32 [1, 4, 512, 10240], P(None, 'row', 'dp', 'col')
- new_row: float32 [1, 4, 512], P(None, 'row', 'dp')
- new_col: float32 [1, 10240], P(None, 'col')
All inputs are finite; a program needn't handle non-finite values.
Results may differ from a plain program's by a relative error of at most 0.0003.
Values sent between devices are 32-bit elements; how exact they have to be, the bound alone decides.
No kernel may reach another device: no remote copies, remote signals or barrier semaphores. Data moves between devices by JAX's collectives and lax.ppermute only.
A program may use at most 64 MiB of HBM per device.

v0:
```python
import jax
import jax.numpy as jnp
from jax import lax
from jax.sharding import PartitionSpec as P

beta_two = 1.0 - 8.0 ** (-0.8)
step_rate = 0.5
tiny_add = 1e-30


def shards(grad_parts, params, row_second, col_second):
    owned_rows = params.shape[2]
    local_cols = params.shape[3]
    slab_rows = row_second.shape[2]
    hidden_width = local_cols * lax.axis_size("col")
    matrix_rows = slab_rows * lax.axis_size("row")
    first_row = lax.axis_index("dp") * owned_rows
    old_owned = lax.dynamic_slice_in_dim(row_second, first_row, owned_rows, 2)
    grad_local = grad_parts[0].astype(jnp.float32)
    gradient = lax.psum_scatter(grad_local, "dp", scatter_dimension=2, tiled=True)
    squares = gradient * gradient + tiny_add
    row_part = jnp.sum(squares, axis=3)
    col_part = jnp.sum(squares, axis=(1, 2))
    row_sum = lax.psum(row_part, "col")
    col_sum = lax.psum(col_part, ("dp", "row"))
    new_row = beta_two * old_owned + (1.0 - beta_two) * (row_sum / hidden_width)
    new_col = beta_two * col_second + (1.0 - beta_two) * (col_sum / matrix_rows)
    row_total = lax.psum(jnp.sum(new_row, axis=(1, 2)), ("dp", "row"))
    row_mean = row_total / matrix_rows
    denominator = new_row[:, :, :, None] * new_col[:, None, None, :] / row_mean[:, None, None, None]
    update = gradient * lax.rsqrt(denominator)
    update_total = lax.psum(jnp.sum(update * update, axis=(1, 2, 3)), ("dp", "row", "col"))
    clip_ratio = jnp.sqrt(update_total / (matrix_rows * hidden_width))
    new_params = params - step_rate * update / jnp.maximum(1.0, clip_ratio)[:, None, None, None]
    return (new_params, new_row, new_col)


def solution(mesh):
    return jax.shard_map(
        shards,
        mesh=mesh,
        in_specs=(
            P("dp", None, "row", None, "col"),
            P(None, "row", "dp", "col"),
            P(None, "row", None),
            P(None, "col"),
        ),
        out_specs=(P(None, "row", "dp", "col"), P(None, "row", "dp"), P(None, "col")),
        check_vma=False,
    )
```

profile of v0, /device:TPU:12, one launch (start us, length us, event | category | flops | bytes accessed | tf_op | source)
XLA Modules:
  0.0 330.2 jit_solution(5967783589630943489)
XLA Ops:
  7.2 0.0 reduce-scatter.2.cloned.1.call-start
  7.2 7.8 %bitcast_convert_fusion = f32[1,1,512,5120]{3,2,1,0:T(8,128)} fusion(bf16[1,1,1,512,5120]{4,3,2,1,0:T(8,128)(2,1)} %param.4), kind=kLoop, calls=%fused_computation | loop fusion | flops 2621440 | bytes 15728640 | tf_op jit(solution)/shard_map/convert_element_type | solution.py:19
  15.0 0.0 reduce-scatter.2.cloned.1.call-update
  15.1 0.0 copy-start.2
  15.1 179.2 %reduce-scatter.2.cloned.1.call-done = f32[1,1,128,5120]{3,2,1,0:T(8,128)} async-done(((f32[1,1,512,5120]{3,2,1,0:T(8,128)}), f32[1,1,128,5120]{3,2,1,0:T(8,128)}) %reduce-scatter.2.cloned.1.call-update) | async-done | bytes 2621456 | tf_op jit(solution)/shard_map/reduce_scatter | solution.py:20
  194.3 0.0 copy-start
  194.3 2.3 fusion
  196.7 2.5 psum.28
  199.1 1.3 fusion.2
  200.4 0.0 copy-start.3
  200.4 66.9 %all-reduce = (f32[1]{0:T(128)}, f32[1,5120]{1,0:T(1,128)S(1)}) all-reduce(f32[1]{0:T(128)} %bitcast.5, f32[1,5120]{1,0:T(1,128)S(1)} %bitcast.13), channel_id=1, replica_groups=mesh['dp'=4,'row'=4,'col'=2] {'dp','row'}, use_global_device_ids=true, to_apply=%region_6.0 | all-reduce | flops 5121 | bytes 40968 | tf_op jit(solution)/shard_map/psum | solution.py:28
  267.9 0.0 copy-done.2
  268.0 0.0 copy-start.1
  268.0 0.0 copy-done
  268.0 1.4 multiply_reduce_fusion
  269.4 49.3 %psum.31 = f32[1]{0:T(128)} all-reduce(f32[1]{0:T(128)} %bitcast.7), channel_id=1, replica_groups=mesh['dp'=4,'row'=4,'col'=2] {'dp','row','col'}, use_global_device_ids=true, to_apply=%region_8.0 | all-reduce | flops 1 | bytes 8 | tf_op jit(solution)/shard_map/psum | solution.py:32
  319.4 3.9 %divide_subtract_fusion = f32[1,1,128,5120]{3,2,1,0:T(8,128)} fusion(f32[1,1,128,5120]{3,2,1,0:T(8,128)} %param.5, f32[]{:T(128)} %bitcast.8, f32[1,1,128,5120]{3,2,1,0:T(8,128)S(1)} %copy-done, f32[]{:T(128)} %bitcast.6, f32[5120]{0:T(1024)S(1)} %bitcast.12, f32[128]{0:T(128)S(1)} %bitcast.15), kind=kLoop, calls=%fused_computation.1 | loop fusion | flops 3932160 | bytes 7885320 | tf_op jit(solution)/shard_map/sub | solution.py:34
  323.3 0.0 copy-done.3
  323.3 0.0 copy-done.1
  (1 shorter events, 0.0 us)
Async XLA Ops:
  7.2 187.2 %reduce-scatter.2.cloned.1.call-start = ((), (), s32[]{:S(2)}) async-start(), calls=%async_computation.1 | async-start | bytes 13107200 | tf_op jit(solution)/shard_map/reduce_scatter | solution.py:20
  15.1 252.8 %copy-start.2 = (f32[1,5120]{1,0:T(1,128)S(1)}, f32[1,5120]{1,0:T(1,128)}, u32[]{:S(2)}) copy-start(f32[1,5120]{1,0:T(1,128)} %param.7) | copy-start | bytes 61444
  194.3 73.6 %copy-start = (f32[1,1,128,5120]{3,2,1,0:T(8,128)S(1)}, f32[1,1,128,5120]{3,2,1,0:T(8,128)}, u32[]{:S(2)}) copy-start(f32[1,1,128,5120]{3,2,1,0:T(8,128)} %reduce-scatter.2.cloned.1.call-done) | copy-start | bytes 7864324
  200.4 122.9 %copy-start.3 = (f32[1,1,128]{2,1,0:T(1,128)}, f32[1,1,128]{2,1,0:T(1,128)S(1)}, u32[]{:S(2)}) copy-start(f32[1,1,128]{2,1,0:T(1,128)S(1)} %get-tuple-element.8) | copy-start | bytes 1540
  268.0 55.4 %copy-start.1 = (f32[1,5120]{1,0:T(1,128)}, f32[1,5120]{1,0:T(1,128)S(1)}, u32[]{:S(2)}) copy-start(f32[1,5120]{1,0:T(1,128)S(1)} %multiply_add_fusion.1) | copy-start | bytes 61444
Sparse Core Ops, SparseCore 0:
  15.2 179.0 reduce-scatter.1
where the time goes:
time: 331 us; the launch traced here: 330 us
  waiting for transfers between devices  179 us (54%)
  blocking collectives  119 us (36%)
  other arithmetic  16.8 us (5%)
  between operations  15.4 us (5%)
    reduce_scatter x1, waiting for transfers between devices, shards(): lax.psum_scatter(grad_local, 'dp', scatter_dimension=2, tiled=True)  179 us
    psum x1, blocking collectives, shards(): row_total = lax.psum(jnp.sum(new_row, axis=(1, 2)), ('dp', 'row'))  66.9 us
    psum x1, blocking collectives, shards(): lax.psum(jnp.sum(update * update, axis=(1, 2, 3)), ('dp', 'row', 'col'))  49.3 us
    convert_element_type x1, other arithmetic, shards(): grad_local = grad_parts[0].astype(jnp.float32)  7.83 us
  transfers between devices with their start and end apart: 1, of which 1 were waited for; matrix products, arithmetic and copies ran while one was open for 0% of the time, Pallas kernels for 0%

commit v1 on v0

--- a/solution.py
+++ b/solution.py
@@ -25,7 +25,7 @@
     col_sum = lax.psum(col_part, ("dp", "row"))
     new_row = beta_two * old_owned + (1.0 - beta_two) * (row_sum / hidden_width)
     new_col = beta_two * col_second + (1.0 - beta_two) * (col_sum / matrix_rows)
-    row_total = lax.psum(jnp.sum(new_row, axis=(1, 2)), ("dp", "row"))
+    row_total = jnp.sum(lax.all_gather(jnp.sum(new_row, axis=(1, 2)), ("dp", "row")), axis=0)
     row_mean = row_total / matrix_rows
     denominator = new_row[:, :, :, None] * new_col[:, None, None, :] / row_mean[:, None, None, None]
     update = gradient * lax.rsqrt(denominator)

time: 331 us -> 333 us (level)
    psum x1 -> x0, blocking collectives: 66.9 us -> none  [shards(): row_total = lax.psum(jnp.sum(new_row, axis=(1, 2)), ('dp', 'row'))]
    unnamed x0 -> x1, blocking collectives: none -> 66.9 us
where the time goes in v1:
time: 333 us; the launch traced here: 332 us
  waiting for transfers between devices  178 us (53%)
  blocking collectives  119 us (36%)
  other arithmetic  17.4 us (5%)
  between operations  15.4 us (5%)
    reduce_scatter x1, waiting for transfers between devices, shards(): lax.psum_scatter(grad_local, 'dp', scatter_dimension=2, tiled=True)  178 us
    unnamed x1, blocking collectives  66.9 us
    psum x1, blocking collectives, shards(): lax.psum(jnp.sum(update * update, axis=(1, 2, 3)), ('dp', 'row', 'col'))  49.3 us
    convert_element_type x1, other arithmetic, shards(): grad_local = grad_parts[0].astype(jnp.float32)  7.83 us
  transfers between devices with their start and end apart: 1, of which 1 were waited for; matrix products, arithmetic and copies ran while one was open for 0% of the time, Pallas kernels for 0%

profile of v1, /device:TPU:12, one launch (start us, length us, event | category | flops | bytes accessed | tf_op | source)
XLA Modules:
  0.0 332.2 jit_solution(5899271284626905070)
XLA Ops:
  7.2 0.0 reduce-scatter.2.cloned.1.call-start
  7.2 7.8 %bitcast_convert_fusion = f32[1,1,512,5120]{3,2,1,0:T(8,128)} fusion(bf16[1,1,1,512,5120]{4,3,2,1,0:T(8,128)(2,1)} %param.4), kind=kLoop, calls=%fused_computation | loop fusion | flops 2621440 | bytes 15728640 | tf_op jit(solution)/shard_map/convert_element_type | solution.py:19
  15.0 0.0 copy-start.4
  15.0 0.0 reduce-scatter.2.cloned.1.call-update
  15.1 0.0 copy-start.2
  15.1 0.6 copy-done.4
  15.7 0.6 dynamic-slice
  16.3 178.1 %reduce-scatter.2.cloned.1.call-done = f32[1,1,128,5120]{3,2,1,0:T(8,128)} async-done(((f32[1,1,512,5120]{3,2,1,0:T(8,128)}), f32[1,1,128,5120]{3,2,1,0:T(8,128)}) %reduce-scatter.2.cloned.1.call-update) | async-done | bytes 2621456 | tf_op jit(solution)/shard_map/reduce_scatter | solution.py:20
  194.3 0.0 copy-start
  194.3 2.3 fusion
  196.7 2.5 psum.21
  199.1 1.3 fusion.2
  200.4 0.0 copy-start.3
  200.4 1.4 dynamic-update-slice
  201.8 66.9 %all-reduce.1 = (f32[16]{0:T(128)S(1)}, f32[1,5120]{1,0:T(1,128)S(1)}) all-reduce(f32[16]{0:T(128)S(1)} %dynamic-update-slice, f32[1,5120]{1,0:T(1,128)S(1)} %bitcast.13), channel_id=1, replica_groups=mesh['dp'=4,'row'=4,'col'=2] {'dp','row'}, use_global_device_ids=true, to_apply=%add | all-reduce | flops 5136 | bytes 41088
  268.6 0.6 reduce.5
  269.9 0.0 copy-done.2
  270.0 0.0 copy-start.1
  270.0 0.0 copy-done
  270.0 1.4 multiply_reduce_fusion
  271.4 49.3 %psum.23 = f32[1]{0:T(128)} all-reduce(f32[1]{0:T(128)} %bitcast.7), channel_id=1, replica_groups=mesh['dp'=4,'row'=4,'col'=2] {'dp','row','col'}, use_global_device_ids=true, to_apply=%region_8.0 | all-reduce | flops 1 | bytes 8 | tf_op jit(solution)/shard_map/psum | solution.py:32
  321.4 3.9 %divide_subtract_fusion = f32[1,1,128,5120]{3,2,1,0:T(8,128)} fusion(f32[1,1,128,5120]{3,2,1,0:T(8,128)} %param.5, f32[]{:T(128)} %bitcast.8, f32[1,1,128,5120]{3,2,1,0:T(8,128)S(1)} %copy-done, f32[]{:T(128)S(6)} %div.36, f32[5120]{0:T(1024)S(1)} %bitcast.12, f32[128]{0:T(128)S(1)} %bitcast.15), kind=kLoop, calls=%fused_computation.1 | loop fusion | flops 3932160 | bytes 7885320 | tf_op jit(solution)/shard_map/sub | solution.py:34
  325.3 0.0 copy-done.3
  325.3 0.0 copy-done.1
  (2 shorter events, 0.0 us)
Async XLA Ops:
  7.2 187.2 %reduce-scatter.2.cloned.1.call-start = ((), (), s32[]{:S(2)}) async-start(), calls=%async_computation.1 | async-start | bytes 13107200 | tf_op jit(solution)/shard_map/reduce_scatter | solution.py:20
  15.0 0.7 copy-start.4
  15.1 254.8 %copy-start.2 = (f32[1,5120]{1,0:T(1,128)S(1)}, f32[1,5120]{1,0:T(1,128)}, u32[]{:S(2)}) copy-start(f32[1,5120]{1,0:T(1,128)} %param.7) | copy-start | bytes 61444
  194.3 75.6 %copy-start = (f32[1,1,128,5120]{3,2,1,0:T(8,128)S(1)}, f32[1,1,128,5120]{3,2,1,0:T(8,128)}, u32[]{:S(2)}) copy-start(f32[1,1,128,5120]{3,2,1,0:T(8,128)} %reduce-scatter.2.cloned.1.call-done) | copy-start | bytes 7864324
  200.4 124.9 %copy-start.3 = (f32[1,1,128]{2,1,0:T(1,128)}, f32[1,1,128]{2,1,0:T(1,128)S(1)}, u32[]{:S(2)}) copy-start(f32[1,1,128]{2,1,0:T(1,128)S(1)} %get-tuple-element.8) | copy-start | bytes 1540
  270.0 55.4 %copy-start.1 = (f32[1,5120]{1,0:T(1,128)}, f32[1,5120]{1,0:T(1,128)S(1)}, u32[]{:S(2)}) copy-start(f32[1,5120]{1,0:T(1,128)S(1)} %multiply_add_fusion.1) | copy-start | bytes 61444
Sparse Core Ops, SparseCore 0:
  15.2 179.0 reduce-scatter.1

commit v2 on v0

--- a/solution.py
+++ b/solution.py
@@ -25,7 +25,7 @@
     col_sum = lax.psum(col_part, ("dp", "row"))
     new_row = beta_two * old_owned + (1.0 - beta_two) * (row_sum / hidden_width)
     new_col = beta_two * col_second + (1.0 - beta_two) * (col_sum / matrix_rows)
-    row_total = lax.psum(jnp.sum(new_row, axis=(1, 2)), ("dp", "row"))
+    row_total = lax.psum(lax.psum(jnp.sum(new_row, axis=(1, 2)), "row"), "dp")
     row_mean = row_total / matrix_rows
     denominator = new_row[:, :, :, None] * new_col[:, None, None, :] / row_mean[:, None, None, None]
     update = gradient * lax.rsqrt(denominator)

time: 331 us -> 348 us (1.051)
  blocking collectives: 119 us -> 136 us
    psum x1 -> x3, blocking collectives: 66.9 us -> 84.6 us  [the longest x1 64.5 us: shards(): col_sum = lax.psum(col_part, ('dp', 'row'))]
where the time goes in v2:
time: 348 us
  waiting for transfers between devices  179 us (51%)
  blocking collectives  136 us (39%)
  other arithmetic  16.8 us (5%)
  between operations  15.4 us (4%)
    reduce_scatter x1, waiting for transfers between devices, shards(): lax.psum_scatter(grad_local, 'dp', scatter_dimension=2, tiled=True)  179 us
    psum x1, blocking collectives, shards(): col_sum = lax.psum(col_part, ('dp', 'row'))  64.5 us
    psum x1, blocking collectives, shards(): lax.psum(jnp.sum(update * update, axis=(1, 2, 3)), ('dp', 'row', 'col'))  49.4 us
    psum x2, blocking collectives, shards(): row_total = lax.psum(lax.psum(jnp.sum(new_row, axis=(1, 2)), 'row'), 'dp')  20.1 us
    convert_element_type x1, other arithmetic, shards(): grad_local = grad_parts[0].astype(jnp.float32)  7.83 us
  transfers between devices with their start and end apart: 1, of which 1 were waited for; matrix products, arithmetic and copies ran while one was open for 0% of the time, Pallas kernels for 0%

profile of v2, /device:TPU:12, one launch (start us, length us, event | category | flops | bytes accessed | tf_op | source)
XLA Modules:
  0.0 347.9 jit_solution(10339860648267952166)
XLA Ops:
  7.2 0.0 reduce-scatter.2.cloned.1.call-start
  7.2 7.8 %bitcast_convert_fusion = f32[1,1,512,5120]{3,2,1,0:T(8,128)} fusion(bf16[1,1,1,512,5120]{4,3,2,1,0:T(8,128)(2,1)} %param.4), kind=kLoop, calls=%fused_computation | loop fusion | flops 2621440 | bytes 15728640 | tf_op jit(solution)/shard_map/convert_element_type | solution.py:19
  15.0 0.0 reduce-scatter.2.cloned.1.call-update
  15.1 0.0 copy-start.2
  15.1 179.2 %reduce-scatter.2.cloned.1.call-done = f32[1,1,128,5120]{3,2,1,0:T(8,128)} async-done(((f32[1,1,512,5120]{3,2,1,0:T(8,128)}), f32[1,1,128,5120]{3,2,1,0:T(8,128)}) %reduce-scatter.2.cloned.1.call-update) | async-done | bytes 2621456 | tf_op jit(solution)/shard_map/reduce_scatter | solution.py:20
  194.3 0.0 copy-start
  194.3 2.3 fusion
  196.7 2.5 psum.35
  199.1 1.3 fusion.2
  200.4 0.0 copy-start.3
  200.4 9.6 %psum.37 = f32[1]{0:T(128)} all-reduce(f32[1]{0:T(128)} %bitcast.5), channel_id=1, replica_groups=mesh['dp'=4,'row'=4,'col'=2] {'row'}, use_global_device_ids=true, to_apply=%region_6.0 | all-reduce | flops 1 | bytes 8 | tf_op jit(solution)/shard_map/psum | solution.py:28
  209.9 10.6 %psum.38 = f32[1]{0:T(128)} all-reduce(f32[1]{0:T(128)} %psum.37), channel_id=1, replica_groups=mesh['dp'=4,'row'=4,'col'=2] {'dp'}, use_global_device_ids=true, to_apply=%region_7.0 | all-reduce | flops 1 | bytes 8 | tf_op jit(solution)/shard_map/psum | solution.py:28
  220.5 64.5 %psum.36 = f32[1,5120]{1,0:T(1,128)S(1)} all-reduce(f32[1,5120]{1,0:T(1,128)S(1)} %bitcast.13), channel_id=1, replica_groups=mesh['dp'=4,'row'=4,'col'=2] {'dp','row'}, use_global_device_ids=true, to_apply=%region_4.0 | all-reduce | flops 5120 | bytes 40960 | tf_op jit(solution)/shard_map/psum | solution.py:25
  285.7 0.0 copy-done.2
  285.7 0.0 copy-start.1
  285.7 0.0 copy-done
  285.8 1.4 multiply_reduce_fusion
  287.1 49.4 %psum.39 = f32[1]{0:T(128)} all-reduce(f32[1]{0:T(128)} %bitcast.7), channel_id=1, replica_groups=mesh['dp'=4,'row'=4,'col'=2] {'dp','row','col'}, use_global_device_ids=true, to_apply=%region_9.0 | all-reduce | flops 1 | bytes 8 | tf_op jit(solution)/shard_map/psum | solution.py:32
  337.2 3.9 %divide_subtract_fusion = f32[1,1,128,5120]{3,2,1,0:T(8,128)} fusion(f32[1,1,128,5120]{3,2,1,0:T(8,128)} %param.5, f32[]{:T(128)} %bitcast.8, f32[1,1,128,5120]{3,2,1,0:T(8,128)S(1)} %copy-done, f32[]{:T(128)} %bitcast.6, f32[5120]{0:T(1024)S(1)} %bitcast.12, f32[128]{0:T(128)S(1)} %bitcast.15), kind=kLoop, calls=%fused_computation.1 | loop fusion | flops 3932160 | bytes 7885320 | tf_op jit(solution)/shard_map/sub | solution.py:34
  341.1 0.0 copy-done.3
  341.1 0.0 copy-done.1
  (1 shorter events, 0.0 us)
Async XLA Ops:
  7.2 187.2 %reduce-scatter.2.cloned.1.call-start = ((), (), s32[]{:S(2)}) async-start(), calls=%async_computation.1 | async-start | bytes 13107200 | tf_op jit(solution)/shard_map/reduce_scatter | solution.py:20
  15.1 270.6 %copy-start.2 = (f32[1,5120]{1,0:T(1,128)S(1)}, f32[1,5120]{1,0:T(1,128)}, u32[]{:S(2)}) copy-start(f32[1,5120]{1,0:T(1,128)} %param.7) | copy-start | bytes 61444
  194.3 91.4 %copy-start = (f32[1,1,128,5120]{3,2,1,0:T(8,128)S(1)}, f32[1,1,128,5120]{3,2,1,0:T(8,128)}, u32[]{:S(2)}) copy-start(f32[1,1,128,5120]{3,2,1,0:T(8,128)} %reduce-scatter.2.cloned.1.call-done) | copy-start | bytes 7864324
  200.4 140.7 %copy-start.3 = (f32[1,1,128]{2,1,0:T(1,128)}, f32[1,1,128]{2,1,0:T(1,128)S(1)}, u32[]{:S(2)}) copy-start(f32[1,1,128]{2,1,0:T(1,128)S(1)} %get-tuple-element.6) | copy-start | bytes 1540
  285.7 55.4 %copy-start.1 = (f32[1,5120]{1,0:T(1,128)}, f32[1,5120]{1,0:T(1,128)S(1)}, u32[]{:S(2)}) copy-start(f32[1,5120]{1,0:T(1,128)S(1)} %multiply_add_fusion.1) | copy-start | bytes 61444
Sparse Core Ops, SparseCore 0:
  15.2 179.0 reduce-scatter.1
